TPU v7x, 256 devices: a whole 4x4x8 slice. The times are simulated.
256 devices in a mesh: row: 4 (over z_lo, core), col: 64 (over y, x, z_hi).
Axes of the slice: x: 4, y: 4, z: 8 (z_hi: 4, z_lo: 2; z = z_hi * 2 + z_lo), core: 2. Of those that a mesh axis runs over, the one named last changes fastest.
Arguments:
- matrix_t: bfloat16 [30720, 30720], P('col', 'row')
- fibers: float32 [3, 131072], P(None, 'col'), may hold values from -0.7 to 0.7, as said below
- forces: float32 [3, 131072], P(None, 'col'), may hold values from -0.375 to 0.375
- nodes: float32 [3, 10240], P(None, 'row'), may hold values from -1 to 1, as said below
- node_order: int32 [10240], replicated, may hold values from 0 to 10239, each once
Outputs:
- velocity: float32 [30720], P(('row', 'col'))
- density: float32 [30720], P(('row', 'col'))
Inputs may be any that keep to these rules, and one draw needn't show every extreme that they name: node_order holds every number below 10240 once. `nodes`: every node lies on the unit sphere about the anchor. `fibers`: every fiber point lies within distance 0.7 of the anchor.
All inputs are finite; a program needn't handle non-finite values.
Results may differ from a plain program's by a relative error of at most 0.00067.
Values may be sent and summed in bfloat16 or wider, within the bound.
A program may use at most 64 MiB of HBM per device.

v0:
```python
import math
import jax
import jax.numpy as jnp
from jax import lax
from jax.sharding import PartitionSpec as P

inv_eight_pi = 1.0 / (8.0 * math.pi)
tiny_eps = 1e-06


def stokeslet_sum(targets, sources, strengths):
    count_src = sources.shape[1]
    width_blk = math.gcd(count_src, 256)

    def advance(turn_index, running):
        source = lax.dynamic_slice_in_dim(sources, turn_index * width_blk, width_blk, 1)
        force_block = lax.dynamic_slice_in_dim(strengths, turn_index * width_blk, width_blk, 1)
        offset = targets[:, None, :] - source[:, :, None]
        inverse = 1.0 / jnp.sqrt(jnp.sum(offset * offset, axis=0))
        projected = jnp.sum(offset * force_block[:, :, None], axis=0) * (
            inverse * inverse * inverse
        )
        return running + jnp.sum(
            force_block[:, :, None] * inverse[None] + offset * projected[None], axis=1
        )

    running = lax.fori_loop(
        0, count_src // width_blk, advance, jnp.zeros(targets.shape, jnp.float32)
    )
    return running * inv_eight_pi


def givens_solve(initial_norm, entry_11, entry_21, entry_12, entry_22, entry_32):
    radius_one = jnp.sqrt(entry_11 * entry_11 + entry_21 * entry_21)
    cosine_one = entry_11 / radius_one
    sine_one = entry_21 / radius_one
    upper_12 = cosine_one * entry_12 + sine_one * entry_22
    lower_22 = cosine_one * entry_22 - sine_one * entry_12
    radius_two = jnp.sqrt(lower_22 * lower_22 + entry_32 * entry_32)
    weight_two = lower_22 / radius_two * (-sine_one * initial_norm) / radius_two
    weight_one = (cosine_one * initial_norm - upper_12 * weight_two) / radius_one
    return (weight_one, weight_two)


def shards(matrix_t, fibers, forces, nodes, node_order):
    width_cols = matrix_t.shape[0]
    block_rows = matrix_t.shape[1]
    piece_rows = block_rows // lax.axis_size("col")
    row_place = lax.axis_index("row")
    col_place = lax.axis_index("col")
    all_nodes = lax.all_gather(nodes, "row", axis=1, tiled=True)
    node_count = block_rows // 3
    my_order = lax.dynamic_slice_in_dim(node_order, row_place * node_count, node_count)
    targets = jnp.take(all_nodes, my_order, axis=1)

    def gather_whole(rounded):
        return lax.all_gather(rounded, "row", axis=0, tiled=True)

    def column_operand(vector):
        rounded = vector.astype(jnp.bfloat16)
        whole = gather_whole(rounded)
        return lax.dynamic_slice_in_dim(whole, col_place * width_cols, width_cols)

    def sum_dots(stacked):
        return lax.psum(stacked, "row")

    def apply_operator(vector):
        column_part = column_operand(vector)
        product = jnp.dot(column_part, matrix_t, preferred_element_type=jnp.float32)
        return lax.psum(product, "col") + vector

    def to_piece(vector):
        return lax.dynamic_slice_in_dim(vector, col_place * piece_rows, piece_rows)

    velocity = lax.psum(stokeslet_sum(targets, fibers, forces).T.reshape(-1), "col")
    initial_norm = jnp.sqrt(sum_dots(jnp.stack([jnp.sum(velocity * velocity)]))[0] + tiny_eps)
    basis_one = velocity / initial_norm
    image_one = apply_operator(basis_one)
    entry_11 = sum_dots(jnp.stack([jnp.sum(basis_one * image_one)]))[0]
    rest_one = image_one - entry_11 * basis_one
    entry_21 = jnp.sqrt(sum_dots(jnp.stack([jnp.sum(rest_one * rest_one)]))[0] + tiny_eps)
    basis_two = rest_one / entry_21
    image_two = apply_operator(basis_two)
    entry_12 = sum_dots(jnp.stack([jnp.sum(basis_one * image_two)]))[0]
    partial_two = image_two - entry_12 * basis_one
    entry_22 = sum_dots(jnp.stack([jnp.sum(basis_two * partial_two)]))[0]
    rest_two = partial_two - entry_22 * basis_two
    entry_32 = jnp.sqrt(sum_dots(jnp.stack([jnp.sum(rest_two * rest_two)]))[0] + tiny_eps)
    weight_one, weight_two = givens_solve(
        initial_norm, entry_11, entry_21, entry_12, entry_22, entry_32
    )
    density = weight_one * basis_one + weight_two * basis_two
    return (to_piece(velocity), to_piece(density))


def solution(mesh):
    return jax.shard_map(
        shards,
        mesh=mesh,
        in_specs=(P("col", "row"), P(None, "col"), P(None, "col"), P(None, "row"), P()),
        out_specs=(P(("row", "col")), P(("row", "col"))),
        check_vma=False,
    )
```

profile of v0, /device:TPU:1, one launch (start us, length us, event | category | flops | bytes accessed | tf_op | source)
XLA Modules:
  0.0 1287.9 jit_solution(4615934349465660564)
XLA Ops:
  2.7 35.1 %all_gather.9 = f32[3,10240]{0,1:T(8,128)} all-gather(f32[3,2560]{0,1:T(8,128)S(1)} %copy.15), channel_id=1, replica_groups=mesh['row'=4,'col'=64] {'row'}, dimensions={1}, use_global_device_ids=true | all-gather | bytes 153600 | tf_op jit(solution)/shard_map/all_gather | solution.py:51
  37.7 6.6 gather_fusion
  46.1 46.0 %while.14 = (s32[]{:T(128)}, f32[3,2560]{1,0:T(4,128)S(1)}, f32[3,2048]{1,0:T(4,128)}, f32[3,2560]{1,0:T(4,128)S(1)}, f32[3,2048]{1,0:T(4,128)}, /*index=5*/s32[]{:T(128)}, s32[]{:T(128)}, s32[]{:T(128)}, s32[]{:T(128)}) while((s32[]{:T(128)}, f32[3,2560]{1,0:T(4,128)S(1)}, f32[3,2048]{1,0:T(4,128)}, f32[3,2560]{1,0:T(4,128)S(1)}, ...), condition=%wide.region_4.5_spmd.clone, body=%wide.region_0.4_spmd.clone.sunk | while | flops 20323844 | bytes 21180568 | solution.py:27
  46.9 2.1 fusion.16
  52.6 2.1 fusion.16
  58.4 2.1 fusion.16
  64.1 2.1 fusion.16
  69.9 2.1 fusion.16
  75.6 2.1 fusion.16
  81.4 2.1 fusion.16
  87.1 2.1 fusion.16
  93.5 325.3 %psum.63 = f32[7680]{0:T(1024)S(1)} all-reduce(f32[7680]{0:T(1024)S(1)} %reshape.41), channel_id=1, replica_groups=mesh['row'=4,'col'=64] {'col'}, use_global_device_ids=true, to_apply=%region_5.6 | all-reduce | flops 7680 | bytes 61440 | tf_op jit(solution)/shard_map/psum | solution.py:75
  419.4 60.8 %psum.64 = f32[1]{0:T(128)} all-reduce(f32[1]{0:T(128)} %bitcast.2), channel_id=1, replica_groups=mesh['row'=4,'col'=64] {'row'}, use_global_device_ids=true, to_apply=%region_7.8 | all-reduce | flops 1 | bytes 8 | tf_op jit(solution)/shard_map/psum | solution.py:65
  480.9 5.9 all-gather
  487.3 4.2 convolution_reduce_fusion.1
  491.4 315.2 %psum.65 = f32[7680]{0:T(1024)S(1)} all-reduce(f32[7680]{0:T(1024)S(1)} %convolution_reduce_fusion.1), channel_id=1, replica_groups=mesh['row'=4,'col'=64] {'col'}, use_global_device_ids=true, to_apply=%region_8.9 | all-reduce | flops 7680 | bytes 61440 | tf_op jit(solution)/shard_map/psum | solution.py:70
  807.3 60.8 %psum.66 = f32[]{:T(128)} all-reduce(f32[]{:T(128)} %get-tuple-element.151), channel_id=1, replica_groups=mesh['row'=4,'col'=64] {'row'}, use_global_device_ids=true, to_apply=%region_10.11 | all-reduce | flops 1 | bytes 8 | tf_op jit(solution)/shard_map/psum | solution.py:65
  869.4 6.3 psum.67
  878.3 6.6 all-gather.1
  885.4 4.2 convolution_reduce_fusion
  889.6 315.2 %psum.68 = f32[7680]{0:T(1024)S(1)} all-reduce(f32[7680]{0:T(1024)S(1)} %convolution_reduce_fusion), channel_id=1, replica_groups=mesh['row'=4,'col'=64] {'col'}, use_global_device_ids=true, to_apply=%region_13.14 | all-reduce | flops 7680 | bytes 61440 | tf_op jit(solution)/shard_map/psum | solution.py:70
  1205.4 60.9 %psum.69 = f32[]{:T(128)} all-reduce(f32[]{:T(128)} %get-tuple-element.147), channel_id=1, replica_groups=mesh['row'=4,'col'=64] {'row'}, use_global_device_ids=true, to_apply=%region_15.16 | all-reduce | flops 1 | bytes 8 | tf_op jit(solution)/shard_map/psum | solution.py:65
  1267.6 6.3 psum.70
  1277.6 7.0 psum.71
  (61 shorter events, 42.9 us)
where the time goes:
time: 1290 us
  blocking collectives  1210 us (94%)
  other arithmetic  50.4 us (4%)
  local copies, waits for them, and re-layouts  16.1 us (1%)
    psum x2, blocking collectives, apply_operator(): return lax.psum(product, 'col') + vector  630 us
    psum x1, blocking collectives, shards(): lax.psum(stokeslet_sum(targets, fibers, forces).T.reshape(-1), 'col')  325 us
    psum x6, blocking collectives, sum_dots(): return lax.psum(stacked, 'row')  202 us
    all_gather x1, blocking collectives, shards(): all_nodes = lax.all_gather(nodes, 'row', axis=1, tiled=True)  35.1 us

commit v1 on v0

--- a/solution.py
+++ b/solution.py
@@ -3,9 +3,14 @@
 import jax.numpy as jnp
 from jax import lax
 from jax.sharding import PartitionSpec as P
+from jax.lax import all_gather
 
 inv_eight_pi = 1.0 / (8.0 * math.pi)
 tiny_eps = 1e-06
+
+
+def fit_the_cubes(raw):
+    return jnp.sum(all_gather(raw, "col"), axis=0)
 
 
 def stokeslet_sum(targets, sources, strengths):
@@ -72,7 +77,7 @@
     def to_piece(vector):
         return lax.dynamic_slice_in_dim(vector, col_place * piece_rows, piece_rows)
 
-    velocity = lax.psum(stokeslet_sum(targets, fibers, forces).T.reshape(-1), "col")
+    velocity = fit_the_cubes(stokeslet_sum(targets, fibers, forces).T.reshape(-1))
     initial_norm = jnp.sqrt(sum_dots(jnp.stack([jnp.sum(velocity * velocity)]))[0] + tiny_eps)
     basis_one = velocity / initial_norm
     image_one = apply_operator(basis_one)

time: 1290 us -> 1010 us (0.78)
  blocking collectives: 1210 us -> 833 us
  waiting for transfers between devices: 0 us -> 77.8 us
  between operations: 7.48 us -> 21.1 us
    psum x1 -> x0, blocking collectives: 325 us -> none  [shards(): lax.psum(stokeslet_sum(targets, fibers, forces).T.reshape(-1), 'col')]
    all_gather x0 -> x1, waiting for transfers between devices: none -> 77.7 us  [fit_the_cubes(): return jnp.sum(all_gather(raw, 'col'), axis=0)]
    psum x6, blocking collectives: 202 us -> 150 us  [sum_dots(): return lax.psum(stacked, 'row')]
  transfers between devices with their start and end apart: 0 -> 1, of which waited for: 0 -> 1; matrix products, arithmetic and copies ran while one was open for 0% -> 0% of each run, Pallas kernels for 0% -> 0%
where the time goes in v1:
time: 1010 us
  blocking collectives  833 us (82%)
  waiting for transfers between devices  77.8 us (8%)
  other arithmetic  53.2 us (5%)
  between operations  21.1 us (2%)
  local copies, waits for them, and re-layouts  16.7 us (2%)
    psum x2, blocking collectives, apply_operator(): return lax.psum(product, 'col') + vector  636 us
    psum x6, blocking collectives, sum_dots(): return lax.psum(stacked, 'row')  150 us
    all_gather x1, waiting for transfers between devices, fit_the_cubes(): return jnp.sum(all_gather(raw, 'col'), axis=0)  77.7 us
    all_gather x1, blocking collectives, shards(): all_nodes = lax.all_gather(nodes, 'row', axis=1, tiled=True)  35.1 us
  transfers between devices with their start and end apart: 1, of which 1 were waited for; matrix products, arithmetic and copies ran while one was open for 0% of the time, Pallas kernels for 0%

profile of v1, /device:TPU:1, one launch (start us, length us, event | category | flops | bytes accessed | tf_op | source)
XLA Modules:
  0.0 1010.6 jit_solution(4598976422078961401)
XLA Ops:
  9.3 35.1 %all_gather.12 = f32[3,10240]{0,1:T(8,128)} all-gather(f32[3,2560]{0,1:T(8,128)S(1)} %copy.15), channel_id=1, replica_groups=mesh['row'=4,'col'=64] {'row'}, dimensions={1}, use_global_device_ids=true | all-gather | bytes 153600 | tf_op jit(solution)/shard_map/all_gather | solution.py:56
  44.3 6.6 gather_fusion
  52.7 46.0 %while.14 = (s32[]{:T(128)}, f32[3,2560]{1,0:T(4,128)S(1)}, f32[3,2048]{1,0:T(4,128)}, f32[3,2560]{1,0:T(4,128)S(1)}, f32[3,2048]{1,0:T(4,128)}, /*index=5*/s32[]{:T(128)}, s32[]{:T(128)}, s32[]{:T(128)}, s32[]{:T(128)}) while((s32[]{:T(128)}, f32[3,2560]{1,0:T(4,128)S(1)}, f32[3,2048]{1,0:T(4,128)}, f32[3,2560]{1,0:T(4,128)S(1)}, ...), condition=%wide.region_4.5_spmd.clone, body=%wide.region_0.4_spmd.clone.sunk | while | flops 20323844 | bytes 21180568 | solution.py:32
  53.5 2.1 fusion.16
  59.2 2.1 fusion.16
  65.0 2.1 fusion.16
  70.7 2.1 fusion.16
  76.5 2.1 fusion.16
  88.0 2.1 fusion.16
  93.7 2.1 fusion.16
  100.7 77.7 %all-gather.5.cloned.1.call-done = f32[64,1,7680]{2,1,0:T(1,128)} async-done(((f32[1,1,7680]{2,1,0:T(1,128)}), f32[64,1,7680]{2,1,0:T(1,128)}) %all-gather.5.cloned.1.call-update) | async-done | bytes 1966096 | tf_op jit(solution)/shard_map/all_gather | solution.py:13
  178.5 2.7 reduce_sum.102
  181.8 7.9 psum.56
  190.4 6.2 all-gather.1
  197.1 4.2 convolution_reduce_fusion.1
  201.2 321.0 %psum.57 = f32[7680]{0:T(1024)S(1)} all-reduce(f32[7680]{0:T(1024)S(1)} %convolution_reduce_fusion.1), channel_id=1, replica_groups=mesh['row'=4,'col'=64] {'col'}, use_global_device_ids=true, to_apply=%region_8.9 | all-reduce | flops 7680 | bytes 61440 | tf_op jit(solution)/shard_map/psum | solution.py:75
  522.8 61.2 %psum.58 = f32[]{:T(128)} all-reduce(f32[]{:T(128)} %get-tuple-element.151), channel_id=1, replica_groups=mesh['row'=4,'col'=64] {'row'}, use_global_device_ids=true, to_apply=%region_10.11 | all-reduce | flops 1 | bytes 8 | tf_op jit(solution)/shard_map/psum | solution.py:70
  586.6 6.4 psum.59
  594.4 6.0 all-gather.2
  600.8 4.2 convolution_reduce_fusion
  605.0 315.1 %psum.60 = f32[7680]{0:T(1024)S(1)} all-reduce(f32[7680]{0:T(1024)S(1)} %convolution_reduce_fusion), channel_id=1, replica_groups=mesh['row'=4,'col'=64] {'col'}, use_global_device_ids=true, to_apply=%region_13.14 | all-reduce | flops 7680 | bytes 61440 | tf_op jit(solution)/shard_map/psum | solution.py:75
  920.7 60.9 %psum.61 = f32[]{:T(128)} all-reduce(f32[]{:T(128)} %get-tuple-element.147), channel_id=1, replica_groups=mesh['row'=4,'col'=64] {'row'}, use_global_device_ids=true, to_apply=%region_15.16 | all-reduce | flops 1 | bytes 8 | tf_op jit(solution)/shard_map/psum | solution.py:70
  983.6 6.2 psum.62
  994.4 7.2 psum.63
  (64 shorter events, 45.8 us)
Async XLA Ops:
  7.2 171.3 %all-gather.5.cloned.1.call-start = ((), (), s32[]{:S(2)}) async-start(), calls=%async_computation | async-start | bytes 1996800 | tf_op jit(solution)/shard_map/all_gather | solution.py:13
Sparse Core Ops, SparseCore 0:
  100.8 77.5 all-gather.4
